TPU v7x, 32 devices: a whole 2x2x4 slice. The times are simulated.
32 devices in a mesh: parts: 2 (over y), tensor: 4 (over z), dp: 4 (over x, core).
Axes of the slice: x: 2, y: 2, z: 4, core: 2. Of those that a mesh axis runs over, the one named last changes fastest.
Arguments:
- inputs: bfloat16 [4096, 8192], P(('parts', 'dp'), 'tensor'), parts along dimension 0, may hold values from -6 to 6
- cotangent: bfloat16 [4096, 8192], P(('parts', 'dp'), 'tensor'), parts along dimension 0, may hold values from -6 to 6
- weight: bfloat16 [8192, 8192], P(None, 'tensor'), may hold values from -0.0625 to 0.0625
- down_weight_maps: bfloat16 [8192, 2048], P('tensor', 'parts'), parts along dimension 1, may hold values from -0.0625 to 0.0625
- up_weight_maps: bfloat16 [2048, 8192], P('parts', 'tensor'), parts along dimension 0, may hold values from -0.75 to 0.75
- counts: int32 [8, 16], P('parts'), parts along dimension 0, may hold values from 0 to 256, as said below
- ranks: int32 [32], P('parts'), parts along dimension 0, may hold values from 8 to 64, as said below
- owners: int32 [32], P('parts'), parts along dimension 0, may hold values from 0 to 3
Outputs:
- projected: bfloat16 [4096, 8192], P(('parts', 'dp'), 'tensor'), parts along dimension 0
- input_grad: bfloat16 [4096, 8192], P(('parts', 'dp'), 'tensor'), parts along dimension 0
- grad_a: float32 [8, 8192, 1024], P(('parts', 'dp'), 'tensor'), parts along dimension 0
- grad_b: float32 [8, 1024, 8192], P(('parts', 'dp'), None, 'tensor'), parts along dimension 0
There are 2 independent parts, one for each index of `parts`. A program takes and returns all parts, laid end to end along the dimension named above; an argument that names none is the same for every part. Nothing has to cross between parts.
Inputs may be any that keep to these rules, and one draw needn't show every extreme that they name: `counts`: each row sums to at most 512, one row to exactly 512, and all rows together to exactly 1024; some entry is exactly 256. `ranks`: each rank is 64 divided by 1, 2, 4 or 8; some trial has 64 and some 64 // 8.
All inputs are finite; a program needn't handle non-finite values.
Results may differ from a plain program's by a relative error of at most 0.0034.
Values may be sent and summed in bfloat16 or wider, within the bound.
A program may use at most 256 MiB of HBM per device.

v0:
```python
import jax
import jax.numpy as jnp
from jax import lax
from jax.sharding import PartitionSpec as P

LARGEST_RANK = 64
TRIALS = 16
LANES = 128
adapter_alpha = 16.0
TRAILING = (((1,), (1,)), ((), ()))
FIRST = (((0,), (0,)), ((), ()))


def fold_columns(values, match):
    width = values.shape[1]
    kept = jnp.where(match, values, 0.0)
    return sum((kept[:, i : i + LANES] for i in range(0, width, LANES)))


def spread_columns(folded, match):
    repeats = match.shape[1] // LANES
    return jnp.where(
        match, jnp.concatenate([folded] * repeats, axis=1), jnp.zeros((), folded.dtype)
    )


def local(inputs, cotangent, weight, down_weight_maps, up_weight_maps, counts, ranks, owners):
    slot_count, feature_local = inputs.shape
    group_count = counts.shape[0]
    width = down_weight_maps.shape[1]
    column = jnp.arange(width, dtype=jnp.int32)
    col_trial = column // LARGEST_RANK
    column_slot = column % LARGEST_RANK
    trial_ids = jnp.arange(TRIALS, dtype=jnp.int32)
    matches = col_trial[:, None] == trial_ids[None, :]
    rank_per_column = jnp.sum(jnp.where(matches, ranks[None, :], 0), axis=1)
    owner_col = jnp.sum(jnp.where(matches, owners[None, :], 0), axis=1)
    scale_per_column = jnp.where(
        column_slot < rank_per_column, adapter_alpha / rank_per_column.astype(jnp.float32), 0.0
    )
    trial_rows = jnp.sum(counts, axis=0)
    per_trial = 1.0 / jnp.maximum(trial_rows, 1).astype(jnp.float32)
    inverse_col = jnp.sum(jnp.where(matches, per_trial[None, :], 0.0), axis=1)
    cumulative = jnp.cumsum(counts, axis=1)
    group_ids = jnp.arange(group_count, dtype=jnp.int32)
    my_group = lax.axis_index("dp")
    positions = jnp.arange(slot_count, dtype=jnp.int32)
    trial_all = jnp.sum(
        (positions[None, :, None] >= cumulative[:, None, :]).astype(jnp.int32), axis=2
    )
    row_trial = jnp.sum(jnp.where((group_ids == my_group)[:, None], trial_all, 0), axis=0)
    is_live = row_trial < TRIALS
    match = row_trial[:, None] == col_trial[None, :]
    match_all = trial_all.reshape(-1)[:, None] == col_trial[None, :]
    coef = jnp.where(match, scale_per_column[None, :], 0.0)
    coef_folded = fold_columns(coef, match)
    down_part = jnp.dot(inputs, down_weight_maps, preferred_element_type=jnp.float32)
    back_part = lax.dot_general(
        cotangent, up_weight_maps, TRAILING, preferred_element_type=jnp.float32
    )
    folded = jnp.concatenate(
        [fold_columns(down_part, match), fold_columns(back_part, match)], axis=1
    )
    folded = lax.psum(folded, "tensor")
    scaled_down_f = (coef_folded * folded[:, :LANES]).astype(jnp.bfloat16)
    scaled_back_f = (coef_folded * folded[:, LANES:]).astype(jnp.bfloat16)
    all_inputs = lax.all_gather(inputs, "tensor", axis=1, tiled=True)
    mine = lax.axis_index("tensor")
    block = jnp.arange(weight.shape[0], dtype=jnp.int32) // feature_local
    frozen_back = lax.dot_general(cotangent, weight, TRAILING, preferred_element_type=jnp.float32)
    others = jnp.where((block == mine)[None, :], 0.0, frozen_back).astype(jnp.bfloat16)
    others_share = lax.psum_scatter(others, "tensor", scatter_dimension=1, tiled=True)
    own_weight = lax.dynamic_slice_in_dim(weight, mine * feature_local, feature_local, 0)
    own_share = lax.dot_general(cotangent, own_weight, TRAILING, preferred_element_type=jnp.float32)
    frozen_share = own_share + others_share.astype(jnp.float32)
    group_inputs = lax.all_gather(inputs, "dp", axis=0, tiled=True)
    group_cotangent = lax.all_gather(cotangent, "dp", axis=0, tiled=True)
    both = lax.all_gather(
        jnp.concatenate([scaled_down_f, scaled_back_f], axis=1), "dp", axis=0, tiled=True
    )
    frozen_output = jnp.dot(all_inputs, weight, preferred_element_type=jnp.float32)
    scaled_down = spread_columns(scaled_down_f, match)
    scaled_back = spread_columns(scaled_back_f, match)
    merged = frozen_output + jnp.dot(
        scaled_down, up_weight_maps, preferred_element_type=jnp.float32
    )
    projected = jnp.where(is_live[:, None], merged, 0.0).astype(jnp.bfloat16)
    adapter_in = lax.dot_general(
        scaled_back, down_weight_maps, TRAILING, preferred_element_type=jnp.float32
    )
    input_grad = jnp.where(is_live[:, None], frozen_share + adapter_in, 0.0).astype(jnp.bfloat16)
    owned = jnp.where(owner_col == my_group, inverse_col, 0.0)
    down_all = spread_columns(both[:, :LANES], match_all)
    back_all = spread_columns(both[:, LANES:], match_all)
    grad_a = lax.dot_general(group_inputs, back_all, FIRST, preferred_element_type=jnp.float32)
    grad_b = lax.dot_general(down_all, group_cotangent, FIRST, preferred_element_type=jnp.float32)
    grad_a = (grad_a * owned[None, :])[None]
    grad_b = (grad_b * owned[:, None])[None]
    return (projected, input_grad, grad_a, grad_b)


def solution(mesh):
    return jax.shard_map(
        local,
        mesh=mesh,
        in_specs=(
            P(("parts", "dp"), "tensor"),
            P(("parts", "dp"), "tensor"),
            P(None, "tensor"),
            P("tensor", "parts"),
            P("parts", "tensor"),
            P("parts", None),
            P("parts"),
            P("parts"),
        ),
        out_specs=(
            P(("parts", "dp"), "tensor"),
            P(("parts", "dp"), "tensor"),
            P(("parts", "dp"), "tensor", None),
            P(("parts", "dp"), None, "tensor"),
        ),
        check_vma=False,
    )
```

profile of v0, /device:TPU:0, one launch (start us, length us, event | category | flops | bytes accessed | tf_op | source)
XLA Modules:
  0.0 511.5 jit_solution(14548352022868119628)
XLA Ops:
  7.2 0.9 reduce_window_sum.11
  8.3 5.3 %compare_select_fusion.4 = f32[512,1024]{1,0:T(8,128)S(1)} fusion(bf16[512,2048]{1,0:T(8,128)(2,1)} %param.9, bf16[1024,2048]{1,0:T(8,128)(2,1)} %param.12, s32[1024]{0:T(1024)S(1)} %add_select_fusion.1, s32[512]{0:T(512)S(1)} %select_reduce_fusion.3), kind=kOutput, calls=%fused_computation.9 | convolution fusion | flops 2148532224 | bytes 8394752 | tf_op jit(solution)/shard_map/dot_general | solution.py:58
  13.8 2.3 compare_select_fusion.5
  16.2 0.8 pad_maximum_fusion
  17.6 40.7 %all-reduce.2.cloned.1.call-done = f32[512,256]{1,0:T(8,128)} async-done(((f32[512,256]{1,0:T(8,128)}), f32[512,256]{1,0:T(8,128)}) %all-reduce.2.cloned.1.call-update) | async-done | bytes 524304 | tf_op jit(solution)/shard_map/psum | solution.py:64
  58.2 1.1 constant_dynamic-update-slice_fusion.15
  59.3 1.8 constant_dynamic-update-slice_fusion.7
  64.0 24.4 %select_convert_fusion = bf16[512,8192]{1,0:T(8,128)(2,1)} fusion(bf16[512,2048]{1,0:T(8,128)(2,1)S(1)} %copy-done.2, bf16[8192,2048]{1,0:T(8,128)(2,1)} %param.10, pred[8192]{0:T(1024)(128)(4,1)S(1)} %fusion.23), kind=kOutput, calls=%fused_computation | convolution fusion | flops 17188257792 | bytes 44048384 | tf_op jit(solution)/shard_map/dot_general | solution.py:70
  89.6 7.7 %fusion.14 = f32[512,2048]{1,0:T(8,128)} fusion(bf16[2048,1024]{1,0:T(8,128)(2,1)} %param.11, bf16[512,1024]{1,0:T(8,128)(2,1)S(1)} %constant_dynamic-update-slice_fusion.8, s32[1024]{0:T(1024)S(1)} %add_select_fusion.1, s32[512]{0:T(512)S(1)} %select_reduce_fusion.3), kind=kOutput, calls=%fused_computation.25 | convolution fusion | flops 2148532224 | bytes 9443328 | tf_op jit(solution)/shard_map/dot_general | solution.py:88
  97.6 4.4 fusion.13
  102.0 2.0 slice_dynamic-update-slice_fusion.6
  104.0 2.0 slice_dynamic-update-slice_fusion.5
  106.0 1.9 slice_dynamic-update-slice_fusion.4
  107.9 1.9 slice_dynamic-update-slice_fusion.3
  109.8 0.9 slice_dynamic-update-slice_fusion.2
  110.6 0.9 slice_dynamic-update-slice_fusion.1
  111.5 0.9 slice_dynamic-update-slice_fusion
  112.4 1.0 slice_dynamic-update-slice_fusion.7
  113.4 0.8 slice_dynamic-update-slice_fusion.13
  114.3 0.8 slice_dynamic-update-slice_fusion.12
  115.1 0.8 slice_dynamic-update-slice_fusion.11
  115.9 0.8 slice_dynamic-update-slice_fusion.10
  116.8 0.8 slice_dynamic-update-slice_fusion.9
  119.2 19.4 %all-gather.9.cloned.1.call-done = bf16[2048,2048]{1,0:T(8,128)(2,1)} async-done(((bf16[512,2048]{1,0:T(8,128)(2,1)}), bf16[2048,2048]{1,0:T(8,128)(2,1)}) %all-gather.9.cloned.1.call-update) | async-done | bytes 8388624 | tf_op jit(solution)/shard_map/all_gather | solution.py:76
  138.6 14.9 %multiply_bitcast_fusion.1 = f32[1,2048,1024]{1,2,0:T(8,128)} fusion(bf16[2048,2048]{1,0:T(8,128)(2,1)} %all-gather.9.cloned.1.call-done, bf16[2048,1024]{1,0:T(8,128)(2,1)} %slice_dynamic-update-slice_fusion.15, f32[1024]{0:T(1024)S(1)} %compare_select_fusion.12, s32[1024]{0:T(1024)S(1)} %add_select_fusion.1, s32[2048]{0:T(1024)S(1)} %bitcast.30), kind=kOutput, calls=%fused_computation.4 | convolution fusion | flops 8596226048 | bytes 20987904 | tf_op jit(solution)/shard_map/dot_general | solution.py:95
  153.5 9.2 %copy.15 = f32[1,2048,1024]{2,1,0:T(8,128)} copy(f32[1,2048,1024]{1,2,0:T(8,128)} %multiply_bitcast_fusion.1) | data formatting | bytes 16777216
  162.7 35.6 %all-gather.11.cloned.1.call-done = bf16[2048,2048]{1,0:T(8,128)(2,1)} async-done(((bf16[512,2048]{1,0:T(8,128)(2,1)}), bf16[2048,2048]{1,0:T(8,128)(2,1)}) %all-gather.11.cloned.1.call-update) | async-done | bytes 8388624 | tf_op jit(solution)/shard_map/all_gather | solution.py:77
  198.3 14.9 %multiply_bitcast_fusion = f32[1,1024,2048]{2,1,0:T(8,128)} fusion(bf16[2048,2048]{1,0:T(8,128)(2,1)} %all-gather.11.cloned.1.call-done, bf16[2048,1024]{1,0:T(8,128)(2,1)} %get-tuple-element.19, f32[1024]{0:T(1024)S(1)} %compare_select_fusion.12, s32[1024]{0:T(1024)S(1)} %add_select_fusion.1, s32[2048]{0:T(1024)S(1)} %bitcast.31), kind=kOutput, calls=%fused_computation.3 | convolution fusion | flops 8596226048 | bytes 20987904 | tf_op jit(solution)/shard_map/dot_general | solution.py:96
  213.2 136.2 %all-gather.5.cloned.1.call-done = bf16[512,8192]{1,0:T(8,128)(2,1)} async-done(((bf16[512,2048]{1,0:T(8,128)(2,1)}), bf16[512,8192]{1,0:T(8,128)(2,1)}) %all-gather.5.cloned.1.call-update) | async-done | bytes 8388624 | tf_op jit(solution)/shard_map/all_gather | solution.py:67
  349.4 24.9 %select_convert_fusion.1 = bf16[512,2048]{1,0:T(8,128)(2,1)} fusion(f32[512,2048]{1,0:T(8,128)} %fusion.13, bf16[512,8192]{1,0:T(8,128)(2,1)} %all-gather.5.cloned.1.call-done, bf16[8192,2048]{1,0:T(8,128)(2,1)} %param.10, pred[512]{0:T(512)(128)(4,1)S(1)} %broadcast_compare_fusion), kind=kOutput, calls=%fused_computation.19 | convolution fusion | flops 17183014912 | bytes 48235008 | tf_op jit(solution)/shard_map/dot_general | solution.py:81
  374.3 120.0 %reduce-scatter.2.cloned.1.call-done = bf16[512,2048]{1,0:T(8,128)(2,1)} async-done(((bf16[512,8192]{1,0:T(8,128)(2,1)}), bf16[512,2048]{1,0:T(8,128)(2,1)}) %reduce-scatter.2.cloned.1.call-update) | async-done | bytes 2097168 | tf_op jit(solution)/shard_map/reduce_scatter | solution.py:72
  494.3 10.3 %fusion.4 = bf16[512,2048]{1,0:T(8,128)(2,1)} fusion(f32[512,2048]{1,0:T(8,128)} %fusion.14, bf16[512,2048]{1,0:T(8,128)(2,1)} %reduce-scatter.2.cloned.1.call-done, bf16[512,2048]{1,0:T(8,128)(2,1)S(1)} %copy-done.2, bf16[8192,2048]{1,0:T(8,128)(2,1)} %param.10, s32[]{:T(128)S(6)} %select_n.128, pred[512]{0:T(512)(128)(4,1)S(1)} %broadcast_compare_fusion), kind=kOutput, calls=%fused_computation.16 | convolution fusion | flops 4300210176 | bytes 18874884 | tf_op jit(solution)/shard_map/dot_general | solution.py:74
  (64 shorter events, 6.7 us)
Async XLA Ops:
  7.2 51.1 %all-reduce.2.cloned.1.call-start = ((), (), s32[]{:S(2)}) async-start(), calls=%async_computation.2 | async-start | bytes 1048576 | tf_op jit(solution)/shard_map/psum | solution.py:64
  8.3 5.5 %copy-start.1 = (bf16[512,2048]{1,0:T(8,128)(2,1)S(1)}, bf16[512,2048]{1,0:T(8,128)(2,1)}, u32[]{:S(2)}) copy-start(bf16[512,2048]{1,0:T(8,128)(2,1)} %param.8) | copy-start | bytes 6291460
  8.3 5.5 %copy-start.7 = (bf16[2048,1024]{1,0:T(8,128)(2,1)S(1)}, bf16[2048,1024]{1,0:T(8,128)(2,1)}, u32[]{:S(2)}) copy-start(bf16[2048,1024]{1,0:T(8,128)(2,1)} %param.11) | copy-start | bytes 12582916
  13.8 3.4 copy-start.5
  13.8 3.4 copy-start.6
  17.1 84.9 %all-gather.7.cloned.1.call-start = ((), (), s32[]{:S(2)}) async-start(), calls=%async_computation.4 | async-start | bytes 1310720 | tf_op jit(solution)/shard_map/all_gather | solution.py:78
  59.3 4.7 copy-start.2
  61.8 76.8 %all-gather.9.cloned.1.call-start = ((), (), s32[]{:S(2)}) async-start(), calls=%async_computation.5 | async-start | bytes 10485760 | tf_op jit(solution)/shard_map/all_gather | solution.py:76
  62.6 135.8 %all-gather.11.cloned.1.call-start = ((), (), s32[]{:S(2)}) async-start(), calls=%async_computation.6 | async-start | bytes 10485760 | tf_op jit(solution)/shard_map/all_gather | solution.py:77
  63.2 286.3 %all-gather.5.cloned.1.call-start = ((), (), s32[]{:S(2)}) async-start(), calls=%async_computation.1 | async-start | bytes 10485760 | tf_op jit(solution)/shard_map/all_gather | solution.py:67
  63.8 430.6 %reduce-scatter.2.cloned.1.call-start = ((), (), s32[]{:S(2)}) async-start(), calls=%async_computation.3 | async-start | bytes 10485760 | tf_op jit(solution)/shard_map/reduce_scatter | solution.py:72
  88.4 0.7 copy-start.4
  89.5 7.7 %copy-start.3 = (bf16[512,1024]{1,0:T(8,128)(2,1)S(1)}, bf16[512,1024]{1,0:T(8,128)(2,1)}, u32[]{:S(2)}) copy-start(bf16[512,1024]{1,0:T(8,128)(2,1)} %get-tuple-element.17) | copy-start | bytes 3145732
  89.5 8.0 %copy-start.8 = (bf16[1024,2048]{1,0:T(8,128)(2,1)S(1)}, bf16[1024,2048]{1,0:T(8,128)(2,1)}, u32[]{:S(2)}) copy-start(bf16[1024,2048]{1,0:T(8,128)(2,1)} %param.12) | copy-start | bytes 12582916
  102.0 7.8 %copy-start = (bf16[2048,256]{1,0:T(8,128)(2,1)S(1)}, bf16[2048,256]{1,0:T(8,128)(2,1)}, u32[]{:S(2)}) copy-start(bf16[2048,256]{1,0:T(8,128)(2,1)} %all-gather.7.cloned.1.call-done) | copy-start | bytes 3145732
Sparse Core Ops, SparseCore 0:
  17.2 40.9 all-reduce.1
  62.0 16.6 all-gather.6
  80.3 58.2 all-gather.8
  140.0 58.2 all-gather.10
  199.8 149.6 all-gather.4
  351.6 142.6 reduce-scatter.1
where the time goes:
time: 512 us; the launch traced here: 511 us
  waiting for transfers between devices  354 us (69%)
  matrix products  109 us (21%)
  local copies, waits for them, and re-layouts  27.7 us (5%)
  between operations  14.4 us (3%)
  other arithmetic  6.18 us (1%)
    all_gather x1, waiting for transfers between devices, local(): all_inputs = lax.all_gather(inputs, 'tensor', axis=1, tiled=True)  136 us
    reduce_scatter x1, waiting for transfers between devices, local(): lax.psum_scatter(others, 'tensor', scatter_dimension=1, tiled=True)  120 us
    psum x1, waiting for transfers between devices, local(): folded = lax.psum(folded, 'tensor')  40.7 us
    all_gather x1, waiting for transfers between devices, local(): group_cotangent = lax.all_gather(cotangent, 'dp', axis=0, tiled=True)  35.6 us
    unnamed x45, local copies, waits for them, and re-layouts  25.8 us
    dot_general x1, matrix products, local(): jnp.dot(all_inputs, weight, preferred_element_type=jnp.float32)  24.9 us
    dot_general x1, matrix products, local(): lax.dot_general(cotangent, weight, TRAILING, preferred_element_type=jnp.f...  24.4 us
    all_gather x1, waiting for transfers between devices, local(): group_inputs = lax.all_gather(inputs, 'dp', axis=0, tiled=True)  19.4 us
  transfers between devices with their start and end apart: 6, of which 5 were waited for; matrix products, arithmetic and copies ran while one was open for 23% of the time, Pallas kernels for 0%

commit v1 on v0

--- a/solution.py
+++ b/solution.py
@@ -61,7 +61,8 @@
     folded = jnp.concatenate(
         [fold_columns(down_part, match), fold_columns(back_part, match)], axis=1
     )
-    folded = lax.psum(folded, "tensor")
+    shards = lax.all_gather(folded, "tensor")
+    folded = jnp.sum(shards, axis=0)
     scaled_down_f = (coef_folded * folded[:, :LANES]).astype(jnp.bfloat16)
     scaled_back_f = (coef_folded * folded[:, LANES:]).astype(jnp.bfloat16)
     all_inputs = lax.all_gather(inputs, "tensor", axis=1, tiled=True)

time: 512 us -> 519 us (1.014)
    all_gather x0 -> x1, waiting for transfers between devices: none -> 48.3 us  [local(): shards = lax.all_gather(folded, 'tensor')]
    psum x1 -> x0, waiting for transfers between devices: 40.7 us -> none  [local(): folded = lax.psum(folded, 'tensor')]
  transfers between devices with their start and end apart: 6 -> 6, of which waited for: 5 -> 5; matrix products, arithmetic and copies ran while one was open for 23% -> 24% of each run, Pallas kernels for 0% -> 0%
where the time goes in v1:
time: 519 us; the launch traced here: 518 us
  waiting for transfers between devices  356 us (69%)
  matrix products  109 us (21%)
  local copies, waits for them, and re-layouts  32.1 us (6%)
  between operations  14.4 us (3%)
  other arithmetic  6.57 us (1%)
    all_gather x1, waiting for transfers between devices, local(): all_inputs = lax.all_gather(inputs, 'tensor', axis=1, tiled=True)  136 us
    reduce_scatter x1, waiting for transfers between devices, local(): lax.psum_scatter(others, 'tensor', scatter_dimension=1, tiled=True)  120 us
    all_gather x1, waiting for transfers between devices, local(): shards = lax.all_gather(folded, 'tensor')  48.3 us
    all_gather x1, waiting for transfers between devices, local(): group_cotangent = lax.all_gather(cotangent, 'dp', axis=0, tiled=True)  35.6 us
    unnamed x45, local copies, waits for them, and re-layouts  29.5 us
    dot_general x1, matrix products, local(): jnp.dot(all_inputs, weight, preferred_element_type=jnp.float32)  24.9 us
    dot_general x1, matrix products, local(): lax.dot_general(cotangent, weight, TRAILING, preferred_element_type=jnp.f...  24.5 us
    dot_general x1, matrix products, local(): lax.dot_general(group_inputs, back_all, FIRST, preferred_element_type=jnp...  14.9 us
  transfers between devices with their start and end apart: 6, of which 5 were waited for; matrix products, arithmetic and copies ran while one was open for 24% of the time, Pallas kernels for 0%

profile of v1, /device:TPU:0, one launch (start us, length us, event | category | flops | bytes accessed | tf_op | source)
XLA Modules:
  0.0 518.2 jit_solution(17458751256449526522)
XLA Ops:
  7.2 0.9 reduce_window_sum.11
  8.3 5.3 %compare_select_fusion.4 = f32[512,1024]{1,0:T(8,128)S(1)} fusion(bf16[512,2048]{1,0:T(8,128)(2,1)} %param.9, bf16[1024,2048]{1,0:T(8,128)(2,1)} %param.12, s32[1024]{0:T(1024)S(1)} %add_select_fusion.1, s32[512]{0:T(512)S(1)} %select_reduce_fusion.3), kind=kOutput, calls=%fused_computation.9 | convolution fusion | flops 2148532224 | bytes 8394752 | tf_op jit(solution)/shard_map/dot_general | solution.py:58
  13.8 2.3 compare_select_fusion.5
  16.2 0.8 pad_maximum_fusion
  17.6 48.3 %all-gather.15.cloned.1.call-done = f32[2048,256]{1,0:T(8,128)} async-done(((f32[512,256]{1,0:T(8,128)}), f32[2048,256]{1,0:T(8,128)}) %all-gather.15.cloned.1.call-update) | async-done | bytes 2097168 | tf_op jit(solution)/shard_map/all_gather | solution.py:64
  65.9 1.8 reduce_sum.66
  72.1 24.5 %select_convert_fusion = bf16[512,8192]{1,0:T(8,128)(2,1)} fusion(bf16[512,2048]{1,0:T(8,128)(2,1)S(1)} %copy-done.2, bf16[8192,2048]{1,0:T(8,128)(2,1)} %param.10, pred[8192]{0:T(1024)(128)(4,1)S(1)} %fusion.23), kind=kOutput, calls=%fused_computation | convolution fusion | flops 17188257792 | bytes 44048384 | tf_op jit(solution)/shard_map/dot_general | solution.py:71
  102.1 7.1 %fusion.14 = f32[512,2048]{1,0:T(8,128)} fusion(bf16[2048,1024]{1,0:T(8,128)(2,1)} %param.11, bf16[512,1024]{1,0:T(8,128)(2,1)} %constant_dynamic-update-slice_fusion.8, s32[1024]{0:T(1024)S(1)} %add_select_fusion.1, s32[512]{0:T(512)S(1)} %select_reduce_fusion.3), kind=kOutput, calls=%fused_computation.25 | convolution fusion | flops 2148532224 | bytes 9443328 | tf_op jit(solution)/shard_map/dot_general | solution.py:89
  109.5 4.4 fusion.13
  113.9 2.0 slice_dynamic-update-slice_fusion.6
  115.9 1.9 slice_dynamic-update-slice_fusion.5
  117.9 1.9 slice_dynamic-update-slice_fusion.4
  119.8 1.9 slice_dynamic-update-slice_fusion.3
  121.7 0.9 slice_dynamic-update-slice_fusion.2
  122.6 0.9 slice_dynamic-update-slice_fusion.1
  123.4 0.9 slice_dynamic-update-slice_fusion
  124.3 1.0 slice_dynamic-update-slice_fusion.7
  125.4 0.8 slice_dynamic-update-slice_fusion.13
  126.2 0.8 slice_dynamic-update-slice_fusion.12
  127.0 0.8 slice_dynamic-update-slice_fusion.11
  127.9 0.8 slice_dynamic-update-slice_fusion.10
  128.7 0.8 slice_dynamic-update-slice_fusion.9
  129.5 0.8 slice_dynamic-update-slice_fusion.8
  131.2 14.2 %all-gather.11.cloned.1.call-done = bf16[2048,2048]{1,0:T(8,128)(2,1)} async-done(((bf16[512,2048]{1,0:T(8,128)(2,1)}), bf16[2048,2048]{1,0:T(8,128)(2,1)}) %all-gather.11.cloned.1.call-update) | async-done | bytes 8388624 | tf_op jit(solution)/shard_map/all_gather | solution.py:77
  145.4 14.9 %multiply_bitcast_fusion.1 = f32[1,2048,1024]{1,2,0:T(8,128)} fusion(bf16[2048,2048]{1,0:T(8,128)(2,1)} %all-gather.11.cloned.1.call-done, bf16[2048,1024]{1,0:T(8,128)(2,1)} %slice_dynamic-update-slice_fusion.15, f32[1024]{0:T(1024)S(1)} %compare_select_fusion.12, s32[1024]{0:T(1024)S(1)} %add_select_fusion.1, s32[2048]{0:T(1024)S(1)} %bitcast.32), kind=kOutput, calls=%fused_computation.4 | convolution fusion | flops 8596226048 | bytes 20987904 | tf_op jit(solution)/shard_map/dot_general | solution.py:96
  160.3 9.2 %copy.15 = f32[1,2048,1024]{2,1,0:T(8,128)} copy(f32[1,2048,1024]{1,2,0:T(8,128)} %multiply_bitcast_fusion.1) | data formatting | bytes 16777216
  169.5 35.6 %all-gather.13.cloned.1.call-done = bf16[2048,2048]{1,0:T(8,128)(2,1)} async-done(((bf16[512,2048]{1,0:T(8,128)(2,1)}), bf16[2048,2048]{1,0:T(8,128)(2,1)}) %all-gather.13.cloned.1.call-update) | async-done | bytes 8388624 | tf_op jit(solution)/shard_map/all_gather | solution.py:78
  205.1 14.9 %multiply_bitcast_fusion = f32[1,1024,2048]{2,1,0:T(8,128)} fusion(bf16[2048,2048]{1,0:T(8,128)(2,1)} %all-gather.13.cloned.1.call-done, bf16[2048,1024]{1,0:T(8,128)(2,1)} %get-tuple-element.19, f32[1024]{0:T(1024)S(1)} %compare_select_fusion.12, s32[1024]{0:T(1024)S(1)} %add_select_fusion.1, s32[2048]{0:T(1024)S(1)} %bitcast.33), kind=kOutput, calls=%fused_computation.3 | convolution fusion | flops 8596226048 | bytes 20987904 | tf_op jit(solution)/shard_map/dot_general | solution.py:97
  220.0 136.2 %all-gather.7.cloned.1.call-done = bf16[512,8192]{1,0:T(8,128)(2,1)} async-done(((bf16[512,2048]{1,0:T(8,128)(2,1)}), bf16[512,8192]{1,0:T(8,128)(2,1)}) %all-gather.7.cloned.1.call-update) | async-done | bytes 8388624 | tf_op jit(solution)/shard_map/all_gather | solution.py:68
  356.2 24.9 %select_convert_fusion.1 = bf16[512,2048]{1,0:T(8,128)(2,1)} fusion(f32[512,2048]{1,0:T(8,128)} %fusion.13, bf16[512,8192]{1,0:T(8,128)(2,1)} %all-gather.7.cloned.1.call-done, bf16[8192,2048]{1,0:T(8,128)(2,1)} %param.10, pred[512]{0:T(512)(128)(4,1)S(1)} %broadcast_compare_fusion), kind=kOutput, calls=%fused_computation.19 | convolution fusion | flops 17183014912 | bytes 48235008 | tf_op jit(solution)/shard_map/dot_general | solution.py:82
  381.1 120.0 %reduce-scatter.2.cloned.1.call-done = bf16[512,2048]{1,0:T(8,128)(2,1)} async-done(((bf16[512,8192]{1,0:T(8,128)(2,1)}), bf16[512,2048]{1,0:T(8,128)(2,1)}) %reduce-scatter.2.cloned.1.call-update) | async-done | bytes 2097168 | tf_op jit(solution)/shard_map/reduce_scatter | solution.py:73
  501.1 10.3 %fusion.4 = bf16[512,2048]{1,0:T(8,128)(2,1)} fusion(f32[512,2048]{1,0:T(8,128)} %fusion.14, bf16[512,2048]{1,0:T(8,128)(2,1)} %reduce-scatter.2.cloned.1.call-done, bf16[512,2048]{1,0:T(8,128)(2,1)S(1)} %copy-done.2, bf16[8192,2048]{1,0:T(8,128)(2,1)} %param.10, s32[]{:T(128)S(6)} %select_n.128, pred[512]{0:T(512)(128)(4,1)S(1)} %broadcast_compare_fusion), kind=kOutput, calls=%fused_computation.16 | convolution fusion | flops 4300210176 | bytes 18874884 | tf_op jit(solution)/shard_map/dot_general | solution.py:75
  (65 shorter events, 11.7 us)
Async XLA Ops:
  7.2 58.7 %all-gather.15.cloned.1.call-start = ((), (), s32[]{:S(2)}) async-start(), calls=%async_computation.6 | async-start | bytes 2621440 | tf_op jit(solution)/shard_map/all_gather | solution.py:64
  8.3 5.5 %copy-start.1 = (bf16[512,2048]{1,0:T(8,128)(2,1)S(1)}, bf16[512,2048]{1,0:T(8,128)(2,1)}, u32[]{:S(2)}) copy-start(bf16[512,2048]{1,0:T(8,128)(2,1)} %param.8) | copy-start | bytes 6291460
  8.3 5.5 %copy-start.7 = (bf16[2048,1024]{1,0:T(8,128)(2,1)S(1)}, bf16[2048,1024]{1,0:T(8,128)(2,1)}, u32[]{:S(2)}) copy-start(bf16[2048,1024]{1,0:T(8,128)(2,1)} %param.11) | copy-start | bytes 12582916
  13.8 3.4 copy-start.5
  13.8 3.4 copy-start.6
  17.1 96.8 %all-gather.9.cloned.1.call-start = ((), (), s32[]{:S(2)}) async-start(), calls=%async_computation.3 | async-start | bytes 1310720 | tf_op jit(solution)/shard_map/all_gather | solution.py:79
  68.5 3.6 copy-start.2
  69.9 75.5 %all-gather.11.cloned.1.call-start = ((), (), s32[]{:S(2)}) async-start(), calls=%async_computation.4 | async-start | bytes 10485760 | tf_op jit(solution)/shard_map/all_gather | solution.py:77
  70.6 134.5 %all-gather.13.cloned.1.call-start = ((), (), s32[]{:S(2)}) async-start(), calls=%async_computation.5 | async-start | bytes 10485760 | tf_op jit(solution)/shard_map/all_gather | solution.py:78
  71.2 285.0 %all-gather.7.cloned.1.call-start = ((), (), s32[]{:S(2)}) async-start(), calls=%async_computation.1 | async-start | bytes 10485760 | tf_op jit(solution)/shard_map/all_gather | solution.py:68
  71.8 429.3 %reduce-scatter.2.cloned.1.call-start = ((), (), s32[]{:S(2)}) async-start(), calls=%async_computation.2 | async-start | bytes 10485760 | tf_op jit(solution)/shard_map/reduce_scatter | solution.py:73
  96.6 0.7 copy-start.4
  102.1 7.1 %copy-start.3 = (bf16[512,1024]{1,0:T(8,128)(2,1)S(1)}, bf16[512,1024]{1,0:T(8,128)(2,1)}, u32[]{:S(2)}) copy-start(bf16[512,1024]{1,0:T(8,128)(2,1)} %get-tuple-element.17) | copy-start | bytes 3145732
  102.1 7.4 %copy-start.8 = (bf16[1024,2048]{1,0:T(8,128)(2,1)S(1)}, bf16[1024,2048]{1,0:T(8,128)(2,1)}, u32[]{:S(2)}) copy-start(bf16[1024,2048]{1,0:T(8,128)(2,1)} %param.12) | copy-start | bytes 12582916
  113.9 7.8 %copy-start = (bf16[2048,256]{1,0:T(8,128)(2,1)S(1)}, bf16[2048,256]{1,0:T(8,128)(2,1)}, u32[]{:S(2)}) copy-start(bf16[2048,256]{1,0:T(8,128)(2,1)} %all-gather.9.cloned.1.call-done) | copy-start | bytes 3145732
Sparse Core Ops, SparseCore 0:
  17.2 48.6 all-gather.14
  70.0 15.4 all-gather.8
  87.1 58.2 all-gather.10
  146.8 58.2 all-gather.12
  206.5 149.6 all-gather.6
  358.4 142.6 reduce-scatter.1
